TPU v7x, 32 devices: a whole 2x2x4 slice. The times are simulated.
32 devices in a mesh: rows: 8 (over y, x, core), tp: 4 (over z).
Axes of the slice: x: 2, y: 2, z: 4, core: 2. Of those that a mesh axis runs over, the one named last changes fastest.
Arguments:
- features: bfloat16 [16384, 768], P('rows'), may hold values from -6 to 6
- type_ids: int32 [16384], P('rows'), may hold values 0 or 1
- segment_ids: int32 [32, 512], P('rows'), may hold values from 0 to 3, never falling along the last dimension, each value on 1 to 256 neighbouring positions
- type_table: bfloat16 [2, 768], replicated, may hold values from -3 to 3
- w_qkv: bfloat16 [3, 768, 768], P(None, None, 'tp'), may hold values from -0.3125 to 0.3125
- b_qv: bfloat16 [2, 768], P(None, 'tp'), may hold values from -3 to 3
- w_out: bfloat16 [768, 768], P('tp'), may hold values from -0.875 to 0.875
- b_out: bfloat16 [768], replicated, may hold values from -3 to 3
- gain_attn: bfloat16 [768], replicated, may hold values from 0.25 to 1.75
- shift_attn: bfloat16 [768], replicated, may hold values from -3 to 3
- w_up: bfloat16 [768, 3072], P(None, 'tp'), may hold values from -0.21875 to 0.21875
- b_up: bfloat16 [3072], P('tp'), may hold values from -3 to 3
- w_down: bfloat16 [3072, 768], P('tp'), may hold values from -0.109375 to 0.109375
- b_down: bfloat16 [768], replicated, may hold values from -3 to 3
- gain_ffn: bfloat16 [768], replicated, may hold values from 0.25 to 1.75
- shift_ffn: bfloat16 [768], replicated, may hold values from -3 to 3
- cotangent: bfloat16 [16384, 768], P('rows'), may hold values from -6 to 6
Outputs:
- output: bfloat16 [16384, 768], P('rows')
- grad_features: bfloat16 [16384, 768], P('rows')
- grad_table: float32 [2, 768], replicated
- grad_qkv: float32 [3, 768, 768], P(None, None, 'tp')
- grad_bias_qv: float32 [2, 768], P(None, 'tp')
- grad_w_out: float32 [768, 768], P('tp')
- grad_b_out: float32 [768], replicated
- grad_gain_attn: float32 [768], replicated
- grad_shift_attn: float32 [768], replicated
- grad_w_up: float32 [768, 3072], P(None, 'tp')
- grad_b_up: float32 [3072], P('tp')
- grad_w_down: float32 [3072, 768], P('tp')
- grad_b_down: float32 [768], replicated
- grad_gain_ffn: float32 [768], replicated
- grad_shift_ffn: float32 [768], replicated
Inputs may be any that keep to these rules, and one draw needn't show every extreme that they name: `segment_ids`: along each packed row the ids never fall; each of the 4 ids covers 1 to 256 tokens, and one covers exactly 256.
All inputs are finite; a program needn't handle non-finite values. No bound on the sum of `type_ids` on one device may be relied on, other than what follows from the above.
Results may differ from a plain program's by a relative error of at most 0.015.
The roundings to bfloat16 on the way count: a program that leaves them out, or rounds other values in their place, can miss the bound.
Values sent between devices are 32-bit elements; how exact they have to be, the bound alone decides.
No kernel may reach another device: no remote copies, remote signals or barrier semaphores. Data moves between devices by JAX's collectives and lax.ppermute only.
A program may use at most 128 MiB of HBM per device.

v0:
```python
from functools import partial
import jax
import jax.numpy as jnp
from jax import lax
from jax.sharding import PartitionSpec as P

HEAD_DIM = 64


def normalize(hidden):
    center = hidden - jnp.mean(hidden, axis=-1, keepdims=True)
    variance = jnp.mean(center * center, axis=-1, keepdims=True)
    inverse = lax.rsqrt(variance + 1e-05)
    return (center * inverse, inverse)


def norm_back(grad_norm, normed, inverse):
    mean_grad = jnp.mean(grad_norm, axis=-1, keepdims=True)
    mean_proj = jnp.mean(grad_norm * normed, axis=-1, keepdims=True)
    return inverse * (grad_norm - mean_grad - normed * mean_proj)


def counted_scores(queries, keys_row, segment):
    scale = queries.shape[-1] ** (-0.5)
    scores = (
        jnp.einsum("qhd,khd->hqk", queries, keys_row, preferred_element_type=jnp.float32) * scale
    )
    same_doc = segment[:, None] == segment[None, :]
    return (jnp.where(same_doc[None], scores, -1000000000.0), scale)


def attend_forward(packed):
    queries, keys_row, values, segment = packed
    masked, scale = counted_scores(queries, keys_row, segment)
    highest_score = jnp.max(masked, axis=-1, keepdims=True)
    weights = jnp.exp(masked - highest_score)
    total = jnp.sum(weights, axis=-1, keepdims=True)
    weights = weights / total
    attended = jnp.einsum(
        "hqk,khd->qhd", weights.astype(jnp.bfloat16), values, preferred_element_type=jnp.float32
    ).astype(jnp.bfloat16)
    return (attended, highest_score[..., 0] + jnp.log(total[..., 0]))


def attend_backward(packed):
    queries, keys_row, values, segment, logsum, grad_attended = packed
    masked, scale = counted_scores(queries, keys_row, segment)
    weights = jnp.exp(masked - logsum[..., None])
    grad_weights = jnp.einsum(
        "qhd,khd->hqk", grad_attended, values, preferred_element_type=jnp.float32
    )
    inner = jnp.sum(weights * grad_weights, axis=-1, keepdims=True)
    grad_scores = (weights * (grad_weights - inner)).astype(jnp.bfloat16)
    grad_queries = (
        jnp.einsum("hqk,khd->qhd", grad_scores, keys_row, preferred_element_type=jnp.float32)
        * scale
    )
    grad_keys = (
        jnp.einsum("hqk,qhd->khd", grad_scores, queries, preferred_element_type=jnp.float32) * scale
    )
    grad_values = jnp.einsum(
        "hqk,qhd->khd",
        weights.astype(jnp.bfloat16),
        grad_attended,
        preferred_element_type=jnp.float32,
    )
    return (grad_queries, grad_keys, grad_values)


def per_device(
    features,
    type_ids,
    segment_ids,
    type_table,
    w_qkv,
    b_qv,
    w_out,
    b_out,
    gain_attn,
    shift_attn,
    w_up,
    b_up,
    w_down,
    b_down,
    gain_ffn,
    shift_ffn,
    cotangent,
):
    tokens = features.shape[0]
    packed_rows = segment_ids.shape[0]
    length = segment_ids.shape[1]
    local_width = w_qkv.shape[2]
    local_heads = local_width // HEAD_DIM
    shape_four = (packed_rows, length, local_heads, HEAD_DIM)
    type_frac = type_ids.astype(jnp.float32)[:, None]
    table = type_table.astype(jnp.float32)
    embedded = features.astype(jnp.float32) + (table[0] + type_frac * (table[1] - table[0]))
    normal_in = embedded.astype(jnp.bfloat16)
    projected = jnp.einsum("nd,sdc->snc", normal_in, w_qkv, preferred_element_type=jnp.float32)
    bias_qv = b_qv.astype(jnp.float32)
    queries = (projected[0] + bias_qv[0]).astype(jnp.bfloat16).reshape(shape_four)
    keys_all = projected[1].astype(jnp.bfloat16).reshape(shape_four)
    values = (projected[2] + bias_qv[1]).astype(jnp.bfloat16).reshape(shape_four)
    attended, logsum = lax.map(attend_forward, (queries, keys_all, values, segment_ids))
    attended = attended.reshape(tokens, local_width)
    attn_part = jnp.dot(attended, w_out, preferred_element_type=jnp.float32)
    attn_out = lax.psum(attn_part, "tp") + b_out.astype(jnp.float32)
    h_one = embedded + attn_out
    normed_a, inverse_a = normalize(h_one)
    gain_one = gain_attn.astype(jnp.float32)
    normed_one = normed_a * gain_one + shift_attn.astype(jnp.float32)
    ffn_in = normed_one.astype(jnp.bfloat16)
    pre_act = jnp.dot(ffn_in, w_up, preferred_element_type=jnp.float32) + b_up.astype(jnp.float32)
    activated = jax.nn.gelu(pre_act, approximate=False).astype(jnp.bfloat16)
    ffn_part = jnp.dot(activated, w_down, preferred_element_type=jnp.float32)
    ffn_out = lax.psum(ffn_part, "tp") + b_down.astype(jnp.float32)
    h_two = normed_one + ffn_out
    normed_b, inverse_b = normalize(h_two)
    gain_two = gain_ffn.astype(jnp.float32)
    output = (normed_b * gain_two + shift_ffn.astype(jnp.float32)).astype(jnp.bfloat16)
    grad_out = cotangent.astype(jnp.float32)
    grad_shift_ffn = jnp.sum(grad_out, axis=0)
    grad_gain_ffn = jnp.sum(grad_out * normed_b, axis=0)
    grad_h2 = norm_back(grad_out * gain_two, normed_b, inverse_b)
    grad_b_down = jnp.sum(grad_h2, axis=0)
    grad_h2_low = grad_h2.astype(jnp.bfloat16)
    grad_w_down = jnp.einsum(
        "nf,nd->fd", activated, grad_h2_low, preferred_element_type=jnp.float32
    )
    grad_act = jnp.einsum("nd,fd->nf", grad_h2_low, w_down, preferred_element_type=jnp.float32)
    unused_value, gelu_pull = jax.vjp(partial(jax.nn.gelu, approximate=False), pre_act)
    grad_pre = gelu_pull(grad_act)[0].astype(jnp.bfloat16)
    grad_b_up = jnp.sum(grad_pre.astype(jnp.float32), axis=0)
    grad_w_up = jnp.einsum("nd,nf->df", ffn_in, grad_pre, preferred_element_type=jnp.float32)
    ffn_grads = (grad_w_up, grad_b_up, grad_w_down, grad_b_down, grad_gain_ffn, grad_shift_ffn)
    grad_in_part = jnp.einsum("nf,df->nd", grad_pre, w_up, preferred_element_type=jnp.float32)
    grad_normed = grad_h2 + lax.psum(grad_in_part, "tp")
    grad_shift_attn = jnp.sum(grad_normed, axis=0)
    grad_gain_attn = jnp.sum(grad_normed * normed_a, axis=0)
    grad_h1 = norm_back(grad_normed * gain_one, normed_a, inverse_a)
    grad_b_out = jnp.sum(grad_h1, axis=0)
    grad_h1_low = grad_h1.astype(jnp.bfloat16)
    grad_w_out = jnp.einsum("nc,nd->cd", attended, grad_h1_low, preferred_element_type=jnp.float32)
    grad_attended = jnp.einsum("nd,cd->nc", grad_h1_low, w_out, preferred_element_type=jnp.float32)
    grad_attended = grad_attended.astype(jnp.bfloat16).reshape(shape_four)
    grad_queries, grad_keys, grad_values = lax.map(
        attend_backward, (queries, keys_all, values, segment_ids, logsum, grad_attended)
    )
    grad_proj = jnp.stack(
        [
            grad_queries.reshape(tokens, local_width),
            grad_keys.reshape(tokens, local_width),
            grad_values.reshape(tokens, local_width),
        ]
    ).astype(jnp.bfloat16)
    grad_bias_qv = jnp.sum(grad_proj[0::2].astype(jnp.float32), axis=1)
    grad_qkv = jnp.einsum("nd,snc->sdc", normal_in, grad_proj, preferred_element_type=jnp.float32)
    grad_embed_part = jnp.einsum(
        "snc,sdc->nd", grad_proj, w_qkv, preferred_element_type=jnp.float32
    )
    grad_embedded = grad_h1 + lax.psum(grad_embed_part, "tp")
    grad_features = grad_embedded.astype(jnp.bfloat16)
    grad_upper = jnp.sum(type_frac * grad_embedded, axis=0)
    grad_lower = jnp.sum(grad_embedded, axis=0) - grad_upper
    grad_table = jnp.stack([grad_lower, grad_upper])
    attn_grads = (
        grad_table,
        grad_qkv,
        grad_bias_qv,
        grad_w_out,
        grad_b_out,
        grad_gain_attn,
        grad_shift_attn,
    )
    summed = lax.psum(
        (
            grad_table,
            grad_qkv,
            grad_bias_qv,
            grad_w_out,
            grad_b_out,
            grad_gain_attn,
            grad_shift_attn,
            grad_w_up,
            grad_b_up,
            grad_w_down,
            grad_b_down,
            grad_gain_ffn,
            grad_shift_ffn,
        ),
        "rows",
    )
    attn_grads = summed[:7]
    ffn_grads = summed[7:]
    return (
        output,
        grad_features,
        attn_grads[0],
        attn_grads[1],
        attn_grads[2],
        attn_grads[3],
        attn_grads[4],
        attn_grads[5],
        attn_grads[6],
        ffn_grads[0],
        ffn_grads[1],
        ffn_grads[2],
        ffn_grads[3],
        ffn_grads[4],
        ffn_grads[5],
    )


def solution(mesh):
    in_specs = (
        P("rows", None),
        P("rows"),
        P("rows", None),
        P(),
        P(None, None, "tp"),
        P(None, "tp"),
        P("tp", None),
        P(),
        P(),
        P(),
        P(None, "tp"),
        P("tp"),
        P("tp", None),
        P(),
        P(),
        P(),
        P("rows", None),
    )
    out_specs = (
        P("rows", None),
        P("rows", None),
        P(),
        P(None, None, "tp"),
        P(None, "tp"),
        P("tp", None),
        P(),
        P(),
        P(),
        P(None, "tp"),
        P("tp"),
        P("tp", None),
        P(),
        P(),
        P(),
    )
    return jax.shard_map(
        per_device, mesh=mesh, in_specs=in_specs, out_specs=out_specs, check_vma=False
    )
```

profile of v0, /device:TPU:0, one launch (start us, length us, event | category | flops | bytes accessed | tf_op | source)
XLA Modules:
  0.0 1206.2 jit_solution(2927941638229971674)
XLA Ops:
  8.8 4.3 fusion.81
  13.0 1.4 fusion.89
  14.5 3.1 squeeze.36
  17.7 2.2 squeeze.37
  22.6 2.9 fusion.66
  25.6 19.1 %while.26 = (s32[]{:T(128)}, bf16[4,512,3,64]{1,3,2,0:T(8,128)(2,1)}, f32[4,3,512]{2,1,0:T(4,128)}, bf16[4,512,3,64]{1,3,2,0:T(8,128)(2,1)S(1)}, s32[4,512]{1,0:...) while((s32[]{:T(128)}, ...), condition=%wide.region_3.4_spmd, body=%wide.region_0.3_spmd.sunk | while | flops 211122688 | bytes 11336281 | solution.py:104
  28.6 1.8 fusion.133
  33.4 1.8 fusion.133
  38.1 1.8 fusion.133
  42.9 1.8 fusion.133
  44.7 1.7 copy.51
  47.5 4.7 fusion.90
  52.4 1.3 convert_element_type.106
  53.7 1.3 convert_element_type.107
  55.0 1.3 convert_element_type.108
  56.2 1.3 convert_element_type.110
  57.5 220.4 %all-reduce.8.cloned.1.call-done = f32[2048,768]{1,0:T(8,128)} async-done(((f32[2048,768]{1,0:T(8,128)}), f32[2048,768]{1,0:T(8,128)}) %all-reduce.8.cloned.1.call-update) | async-done | bytes 6291472 | tf_op jit(solution)/shard_map/psum | solution.py:107
  277.9 4.8 fusion.88
  285.4 18.4 %multiply_convert_fusion.1 = (bf16[2048,768]{1,0:T(8,128)(2,1)S(1)}, f32[2048,768]{1,0:T(8,128)}, f32[2048,768]{1,0:T(8,128)}) fusion(f32[768]{0:T(1024)S(1)} %copy-done.38, bf16[2048,768]{1,0:T(8,128)(2,1)S(1)} %fusion.63, bf16[768,768]{1,0:T(8,128)(2,1)S(1)} %copy-done), kind=kOutput, calls=%fused_computation.80 | convolution fusion | flops 2519728128 | bytes 20057088 | tf_op jit(solution)/shard_map/dot_general | solution.py:113
  303.8 1.6 copy-done.10
  305.5 4.6 fusion.91
  310.1 1.3 convert_element_type.112
  311.4 1.3 convert_element_type.113
  312.6 1.3 convert_element_type.114
  313.9 218.0 %all-reduce.10.cloned.1.call-done = f32[2048,768]{1,0:T(8,128)} async-done(((f32[2048,768]{1,0:T(8,128)}), f32[2048,768]{1,0:T(8,128)}) %all-reduce.10.cloned.1.call-update) | async-done | bytes 6291472 | tf_op jit(solution)/shard_map/psum | solution.py:116
  531.9 5.7 fusion.86
  539.5 3.6 fusion.56
  543.2 4.5 fusion.84
  547.7 9.5 convert_reduce_fusion.1
  557.2 1.8 copy-done.42
  559.0 4.5 fusion.92
  563.8 221.6 %all-reduce.12.cloned.1.call-done = f32[2048,768]{1,0:T(8,128)} async-done(((f32[2048,768]{1,0:T(8,128)}), f32[2048,768]{1,0:T(8,128)}) %all-reduce.12.cloned.1.call-update) | async-done | bytes 6291472 | tf_op jit(solution)/shard_map/psum | solution.py:137
  785.4 8.7 multiply_reduce_fusion.1
  794.2 4.5 subtract_multiply_fusion
  798.7 2.6 copy-done.3
  801.4 1.2 convolution_convert_fusion
  802.6 1.5 reshape.196
  804.0 1.3 copy.53
  805.3 30.2 %while.27 = (s32[]{:T(128)}, bf16[4,512,3,64]{1,3,2,0:T(8,128)(2,1)}, bf16[4,512,3,64]{1,3,2,0:T(8,128)(2,1)}, bf16[4,512,3,64]{1,3,2,0:T(8,128)(2,1)}, bf16[4,5...) while((s32[]{:T(128)}, ...), condition=%wide.region_17.18_spmd, body=%wide.region_15.17_spmd.sunk | while | flops 510851584 | bytes 39300324 | solution.py:146
  807.6 1.2 multiply_reduce_fusion.8
  811.5 1.3 fusion.145
  815.0 1.2 multiply_reduce_fusion.8
  819.0 1.3 fusion.145
  822.5 1.2 multiply_reduce_fusion.8
  826.4 1.3 fusion.145
  829.9 1.2 multiply_reduce_fusion.8
  833.9 1.3 fusion.145
  835.5 1.7 copy.54
  838.8 1.7 copy.55
  841.2 1.7 copy.56
  845.4 7.1 convolution_bitcast_fusion
  852.8 7.1 fusion.93
  859.9 7.0 fusion.71
  866.9 4.5 fusion.68
  871.5 3.5 fusion.77
  875.0 1.6 copy-done.13
  877.0 197.4 %all-reduce.14.cloned.1.call-done = f32[2048,768]{1,0:T(8,128)} async-done(((f32[2048,768]{1,0:T(8,128)}), f32[2048,768]{1,0:T(8,128)}) %all-reduce.14.cloned.1.call-update) | async-done | bytes 6291472 | tf_op jit(solution)/shard_map/psum | solution.py:161
  1074.5 6.9 add_reduce_fusion
  1081.5 27.2 %all-reduce = (f32[2,768]{1,0:T(2,128)}, f32[2,192]{1,0:T(2,128)}, f32[768]{0:T(1024)}, f32[768]{0:T(1024)}, f32[768]{0:T(1024)}, /*index=5*/f32[768]{0:T(1024)}, f32[768]{0:T(1024)}, f32[768]{0:T(1024)}, f32[768]{0:T(1024)}) all-reduce(f32[2,768]{1,0:T(2,128)S(1)} %pad_maximum_fusion, ...), channel_id=1, replica_groups=mesh['rows'=8,'tp'=4] {'rows'}, use_global_device_ids=true, to_apply=%region_21.22 | all-reduce | flops 7296 | bytes 58368 | tf_op jit(solution)/shard_map/psum | solution.py:175
  1108.7 83.1 %all-reduce.16.cloned.1.call-done = (f32[3,768,192]{1,2,0:T(8,128)}, f32[192,768]{1,0:T(8,128)}, f32[768,768]{1,0:T(8,128)}, f32[768,768]{1,0:T(8,128)}) async-done(((f32[3,768,192]{1,2,0:T(8,128)}, f32[192,768]{1,0:T(8,128)}, f32[768,768]{1,0:T(8,128)}, f32[768,768]{1,0:T(8,128)}), (f32[3,768,192]{1,2,0:T(8,128)}, f32[192,768]{1,0:T(8,128)}, f32[768,768]{1,0:T(8,128)}, ...) | async-done | bytes 7077904 | tf_op jit(solution)/shard_map/psum | solution.py:175
  1191.8 2.9 copy.106
  1194.7 1.9 copy.107
  1196.7 1.4 copy.108
  1198.1 1.4 copy.109
  (206 shorter events, 47.6 us)
Async XLA Ops:
  7.2 278.2 %copy-start = (bf16[768,768]{1,0:T(8,128)(2,1)S(1)}, bf16[768,768]{1,0:T(8,128)(2,1)}, u32[]{:S(2)}) copy-start(bf16[768,768]{1,0:T(8,128)(2,1)} %param.31) | copy-start | bytes 3538948
  7.2 270.7 %all-reduce.8.cloned.1.call-start = ((), (), s32[]{:S(2)}) async-start(), calls=%async_computation | async-start | bytes 12582912 | tf_op jit(solution)/shard_map/psum | solution.py:107
  8.0 269.9 %copy-start.29 = (f32[768]{0:T(1024)}, f32[768]{0:T(1024)S(1)}, u32[]{:S(2)}) copy-start(f32[768]{0:T(1024)S(1)} %get-tuple-element.157) | copy-start | bytes 9220
  8.1 269.9 %copy-start.31 = (f32[768]{0:T(1024)}, f32[768]{0:T(1024)S(1)}, u32[]{:S(2)}) copy-start(f32[768]{0:T(1024)S(1)} %get-tuple-element.158) | copy-start | bytes 9220
  8.8 269.2 %copy-start.23 = (f32[2048]{0:T(1024)}, f32[2048]{0:T(1024)S(1)}, u32[]{:S(2)}) copy-start(f32[2048]{0:T(1024)S(1)} %convert_element_type.100) | copy-start | bytes 24580
  46.6 0.9 copy-start.6
  52.2 479.7 %all-reduce.10.cloned.1.call-start = ((), (), s32[]{:S(2)}) async-start(), calls=%async_computation.1 | async-start | bytes 12582912 | tf_op jit(solution)/shard_map/psum | solution.py:116
  282.7 2.7 copy-start.2
  282.7 0.9 copy-start.21
  282.7 0.9 copy-start.26
  283.6 1.8 copy-start.38
  285.4 18.5 %copy-start.9 = (bf16[2048,768]{1,0:T(8,128)(2,1)}, bf16[2048,768]{1,0:T(8,128)(2,1)S(1)}, u32[]{:S(2)}) copy-start(bf16[2048,768]{1,0:T(8,128)(2,1)S(1)} %fusion.63) | copy-start | bytes 9437188
  285.4 20.1 %copy-start.40 = (bf16[768,768]{1,0:T(8,128)(2,1)S(1)}, bf16[768,768]{1,0:T(8,128)(2,1)}, u32[]{:S(2)}) copy-start(bf16[768,768]{1,0:T(8,128)(2,1)} %param.33) | copy-start | bytes 3538948
  303.8 1.6 copy-start.10
  310.0 475.4 %all-reduce.12.cloned.1.call-start = ((), (), s32[]{:S(2)}) async-start(), calls=%async_computation.2 | async-start | bytes 12582912 | tf_op jit(solution)/shard_map/psum | solution.py:137
  537.6 1.9 copy-start.5
  537.7 1.9 copy-start.25
  538.5 4.6 copy-start.36
  539.5 8.1 slice-start
  543.2 4.5 copy-start.39
  543.2 4.5 copy-start.41
  543.2 4.5 slice-start.1
  547.7 9.5 copy-start.4
  557.2 1.8 copy-start.42
  563.5 221.9 %copy-start.22 = (f32[768]{0:T(1024)S(1)}, f32[768]{0:T(1024)}, u32[]{:S(2)}) copy-start(f32[768]{0:T(1024)} %convert_element_type.107) | copy-start | bytes 9220
  563.5 510.9 %all-reduce.14.cloned.1.call-start = ((), (), s32[]{:S(2)}) async-start(), calls=%async_computation.3 | async-start | bytes 12582912 | tf_op jit(solution)/shard_map/psum | solution.py:161
  794.2 7.2 copy-start.16
  798.7 2.7 copy-start.3
  807.6 2.0 copy-start.19
  808.7 1.5 copy-start.17
  810.2 1.3 copy-start.20
  810.6 0.9 copy-start.18
  815.0 2.0 copy-start.19
  816.2 1.5 copy-start.17
  817.7 1.3 copy-start.20
  818.1 0.9 copy-start.18
  822.5 2.0 copy-start.19
  823.6 1.5 copy-start.17
  825.1 1.3 copy-start.20
  825.5 0.9 copy-start.18
  829.9 2.0 copy-start.19
  831.1 1.5 copy-start.17
  832.6 1.3 copy-start.20
  833.0 0.9 copy-start.18
  852.6 339.2 %all-reduce.16.cloned.1.call-start = ((), (), s32[]{:S(2)}) async-start(), calls=%async_computation.4 | async-start | bytes 14155776 | tf_op jit(solution)/shard_map/psum | solution.py:175
  852.8 7.1 copy-start.11
  859.9 7.1 copy-start.7
  866.9 4.6 copy-start.8
  866.9 4.6 copy-start.12
  866.9 4.6 copy-start.24
  866.9 4.6 copy-start.30
  866.9 4.6 copy-start.32
  875.0 1.7 copy-start.13
  877.0 204.4 %copy-start.27 = (f32[768]{0:T(1024)S(1)}, f32[768]{0:T(1024)}, u32[]{:S(2)}) copy-start(f32[768]{0:T(1024)} %get-tuple-element.150) | copy-start | bytes 9220
  877.0 204.4 %copy-start.28 = (f32[768]{0:T(1024)S(1)}, f32[768]{0:T(1024)}, u32[]{:S(2)}) copy-start(f32[768]{0:T(1024)} %get-tuple-element.156) | copy-start | bytes 9220
  877.0 204.4 %copy-start.33 = (f32[768]{0:T(1024)S(1)}, f32[768]{0:T(1024)}, u32[]{:S(2)}) copy-start(f32[768]{0:T(1024)} %get-tuple-element.208) | copy-start | bytes 9220
  877.0 204.4 %copy-start.34 = (f32[768]{0:T(1024)S(1)}, f32[768]{0:T(1024)}, u32[]{:S(2)}) copy-start(f32[768]{0:T(1024)} %get-tuple-element.146) | copy-start | bytes 9220
  877.0 204.4 %copy-start.35 = (f32[768]{0:T(1024)S(1)}, f32[768]{0:T(1024)}, u32[]{:S(2)}) copy-start(f32[768]{0:T(1024)} %get-tuple-element.153) | copy-start | bytes 9220
  877.0 204.4 %copy-start.37 = (f32[768]{0:T(1024)S(1)}, f32[768]{0:T(1024)}, u32[]{:S(2)}) copy-start(f32[768]{0:T(1024)} %get-tuple-element.226) | copy-start | bytes 9220
  1191.8 4.9 copy-start.15
  1191.8 6.3 copy-start.14
  1191.8 7.7 copy-start.1
Sparse Core Ops, SparseCore 0:
  52.3 225.5 all-reduce.7
  310.2 221.7 all-reduce.9
  563.6 221.7 all-reduce.11
  852.7 221.7 all-reduce.13
  1079.1 112.6 all-reduce.15
where the time goes:
time: 1220 us; the launch traced here: 1210 us
  waiting for transfers between devices  941 us (77%)
  matrix products  103 us (8%)
  other arithmetic  66.3 us (5%)
  local copies, waits for them, and re-layouts  53.4 us (4%)
  blocking collectives  27.2 us (2%)
  between operations  14.5 us (1%)
    psum x1, waiting for transfers between devices, per_device(): grad_normed = grad_h2 + lax.psum(grad_in_part, 'tp')  222 us
    psum x1, waiting for transfers between devices, per_device(): attn_out = lax.psum(attn_part, 'tp') + b_out.astype(jnp.float32)  220 us
    psum x1, waiting for transfers between devices, per_device(): ffn_out = lax.psum(ffn_part, 'tp') + b_down.astype(jnp.float32)  218 us
    psum x1, waiting for transfers between devices, per_device(): grad_embedded = grad_h1 + lax.psum(grad_embed_part, 'tp')  197 us
    psum x1, waiting for transfers between devices, per_device(): lax.psum((grad_table, grad_qkv, grad_bias_qv, grad_w_out, grad_b_out, gra...  83.1 us
    psum x1, blocking collectives, per_device(): lax.psum((grad_table, grad_qkv, grad_bias_qv, grad_w_out, grad_b_out, gra...  27.2 us
  transfers between devices with their start and end apart: 5, of which 5 were waited for; matrix products, arithmetic and copies ran while one was open for 3% of the time, Pallas kernels for 0%

commit v1 on v0

--- a/solution.py
+++ b/solution.py
@@ -104,7 +104,7 @@
     attended, logsum = lax.map(attend_forward, (queries, keys_all, values, segment_ids))
     attended = attended.reshape(tokens, local_width)
     attn_part = jnp.dot(attended, w_out, preferred_element_type=jnp.float32)
-    attn_out = lax.psum(attn_part, "tp") + b_out.astype(jnp.float32)
+    attn_out = lax.all_gather(attn_part, "tp").sum(axis=0) + b_out.astype(jnp.float32)
     h_one = embedded + attn_out
     normed_a, inverse_a = normalize(h_one)
     gain_one = gain_attn.astype(jnp.float32)

time: 1220 us -> 1430 us (1.17)
  waiting for transfers between devices: 941 us -> 1150 us
    all_gather x0 -> x1, waiting for transfers between devices: none -> 427 us  [per_device(): lax.all_gather(attn_part, 'tp').sum(axis=0) + b_out.astype(jnp.float32)]
    psum x1 -> x0, waiting for transfers between devices: 220 us -> none  [per_device(): attn_out = lax.psum(attn_part, 'tp') + b_out.astype(jnp.float32)]
  transfers between devices with their start and end apart: 5 -> 5, of which waited for: 5 -> 5; matrix products, arithmetic and copies ran while one was open for 3% -> 2% of each run, Pallas kernels for 0% -> 0%
where the time goes in v1:
time: 1430 us; the launch traced here: 1420 us
  waiting for transfers between devices  1150 us (80%)
  matrix products  106 us (7%)
  other arithmetic  70 us (5%)
  local copies, waits for them, and re-layouts  47 us (3%)
  blocking collectives  27.2 us (2%)
  between operations  14.8 us (1%)
    all_gather x1, waiting for transfers between devices, per_device(): lax.all_gather(attn_part, 'tp').sum(axis=0) + b_out.astype(jnp.float32)  427 us
    psum x1, waiting for transfers between devices, per_device(): grad_normed = grad_h2 + lax.psum(grad_in_part, 'tp')  222 us
    psum x1, waiting for transfers between devices, per_device(): ffn_out = lax.psum(ffn_part, 'tp') + b_down.astype(jnp.float32)  220 us
    psum x1, waiting for transfers between devices, per_device(): grad_embedded = grad_h1 + lax.psum(grad_embed_part, 'tp')  199 us
    psum x1, waiting for transfers between devices, per_device(): lax.psum((grad_table, grad_qkv, grad_bias_qv, grad_w_out, grad_b_out, gra...  83.1 us
  transfers between devices with their start and end apart: 5, of which 5 were waited for; matrix products, arithmetic and copies ran while one was open for 2% of the time, Pallas kernels for 0%

profile of v1, /device:TPU:0, one launch (start us, length us, event | category | flops | bytes accessed | tf_op | source)
XLA Modules:
  0.0 1419.1 jit_solution(12289100574777248695)
XLA Ops:
  8.8 4.3 fusion.81
  13.0 1.4 fusion.89
  14.6 3.1 squeeze.36
  17.8 2.2 squeeze.37
  22.7 2.9 fusion.66
  25.7 16.3 %while.26 = (s32[]{:T(128)}, bf16[4,512,3,64]{1,3,2,0:T(8,128)(2,1)}, f32[4,3,512]{2,1,0:T(4,128)}, bf16[4,512,3,64]{1,3,2,0:T(8,128)(2,1)S(1)}, s32[4,512]{1,0:...) while((s32[]{:T(128)}, ...), condition=%wide.region_3.4_spmd, body=%wide.region_0.3_spmd.sunk | while | flops 211122688 | bytes 11336281 | solution.py:104
  28.0 1.8 fusion.133
  32.1 1.8 fusion.133
  36.2 1.8 fusion.133
  40.3 1.8 fusion.133
  42.0 2.0 copy.51
  45.1 4.7 fusion.90
  50.6 427.3 %all-gather.3.cloned.1.call-done = f32[8192,768]{1,0:T(8,128)} async-done(((f32[2048,768]{1,0:T(8,128)}), f32[8192,768]{1,0:T(8,128)}) %all-gather.3.cloned.1.call-update) | async-done | bytes 25165840 | tf_op jit(solution)/shard_map/all_gather | solution.py:107
  477.9 12.7 reduce_sum.193
  490.6 4.7 fusion.88
  496.3 1.1 fusion.63
  498.0 18.4 %multiply_convert_fusion.1 = (bf16[2048,768]{1,0:T(8,128)(2,1)S(1)}, f32[2048,768]{1,0:T(8,128)}, f32[2048,768]{1,0:T(8,128)}) fusion(f32[768]{0:T(1024)S(1)} %convert_element_type.110, bf16[2048,768]{1,0:T(8,128)(2,1)S(1)} %fusion.63, bf16[768,768]{1,0:T(8,128)(2,1)S(1)} %copy-done), kind=kOutput, calls=%fused_computation.80 | convolution fusion | flops 2519728128 | bytes 20057088 | tf_op jit(solution)/shard_map/dot_general | solution.py:113
  516.5 1.6 copy-done.10
  518.1 4.6 fusion.91
  523.4 220.5 %all-reduce.7.cloned.1.call-done = f32[2048,768]{1,0:T(8,128)} async-done(((f32[2048,768]{1,0:T(8,128)}), f32[2048,768]{1,0:T(8,128)}) %all-reduce.7.cloned.1.call-update) | async-done | bytes 6291472 | tf_op jit(solution)/shard_map/psum | solution.py:116
  743.9 5.7 fusion.86
  750.5 1.0 copy-done.4
  751.5 3.6 fusion.56
  755.1 4.5 fusion.84
  759.6 9.5 convert_reduce_fusion.1
  769.1 1.8 copy-done.44
  770.9 4.5 fusion.92
  775.7 221.6 %all-reduce.9.cloned.1.call-done = f32[2048,768]{1,0:T(8,128)} async-done(((f32[2048,768]{1,0:T(8,128)}), f32[2048,768]{1,0:T(8,128)}) %all-reduce.9.cloned.1.call-update) | async-done | bytes 6291472 | tf_op jit(solution)/shard_map/psum | solution.py:137
  997.3 8.7 multiply_reduce_fusion.1
  1006.1 4.5 subtract_multiply_fusion
  1010.6 2.6 copy-done.2
  1013.3 1.2 convolution_convert_fusion
  1014.5 1.5 reshape.196
  1016.0 1.3 copy.53
  1017.2 31.0 %while.27 = (s32[]{:T(128)}, bf16[4,512,3,64]{1,3,2,0:T(8,128)(2,1)}, bf16[4,512,3,64]{1,3,2,0:T(8,128)(2,1)}, bf16[4,512,3,64]{1,3,2,0:T(8,128)(2,1)}, bf16[4,5...) while((s32[]{:T(128)}, ...), condition=%wide.region_17.18_spmd, body=%wide.region_15.17_spmd.sunk | while | flops 510851584 | bytes 39300324 | solution.py:146
  1017.3 1.5 fusion.142
  1019.8 1.2 multiply_reduce_fusion.8
  1023.7 1.3 fusion.145
  1024.9 1.5 fusion.142
  1027.4 1.2 multiply_reduce_fusion.8
  1031.4 1.3 fusion.145
  1032.6 1.5 fusion.142
  1035.1 1.2 multiply_reduce_fusion.8
  1039.0 1.3 fusion.145
  1040.3 1.5 fusion.142
  1042.8 1.2 multiply_reduce_fusion.8
  1046.7 1.3 fusion.145
  1048.2 1.7 copy.54
  1051.5 1.7 copy.55
  1053.8 1.7 copy.56
  1056.2 0.9 constant_dynamic-update-slice_fusion.1
  1058.0 7.1 convolution_bitcast_fusion
  1065.5 7.1 fusion.93
  1072.6 7.0 fusion.71
  1079.7 4.6 fusion.68
  1084.3 3.5 fusion.77
  1088.2 198.9 %all-reduce.11.cloned.1.call-done = f32[2048,768]{1,0:T(8,128)} async-done(((f32[2048,768]{1,0:T(8,128)}), f32[2048,768]{1,0:T(8,128)}) %all-reduce.11.cloned.1.call-update) | async-done | bytes 6291472 | tf_op jit(solution)/shard_map/psum | solution.py:161
  1287.1 6.9 add_reduce_fusion
  1294.1 27.2 %all-reduce = (f32[2,768]{1,0:T(2,128)}, f32[2,192]{1,0:T(2,128)}, f32[768]{0:T(1024)}, f32[768]{0:T(1024)}, f32[768]{0:T(1024)}, /*index=5*/f32[768]{0:T(1024)}, f32[768]{0:T(1024)}, f32[768]{0:T(1024)}, f32[768]{0:T(1024)}) all-reduce(f32[2,768]{1,0:T(2,128)S(1)} %pad_maximum_fusion, ...), channel_id=1, replica_groups=mesh['rows'=8,'tp'=4] {'rows'}, use_global_device_ids=true, to_apply=%region_21.22 | all-reduce | flops 7296 | bytes 58368 | tf_op jit(solution)/shard_map/psum | solution.py:175
  1321.3 83.1 %all-reduce.13.cloned.1.call-done = (f32[3,768,192]{1,2,0:T(8,128)}, f32[192,768]{1,0:T(8,128)}, f32[768,768]{1,0:T(8,128)}, f32[768,768]{1,0:T(8,128)}) async-done(((f32[3,768,192]{1,2,0:T(8,128)}, f32[192,768]{1,0:T(8,128)}, f32[768,768]{1,0:T(8,128)}, f32[768,768]{1,0:T(8,128)}), (f32[3,768,192]{1,2,0:T(8,128)}, f32[192,768]{1,0:T(8,128)}, f32[768,768]{1,0:T(8,128)}, ...) | async-done | bytes 7077904 | tf_op jit(solution)/shard_map/psum | solution.py:175
  1404.4 2.9 copy.105
  1407.4 1.9 copy.106
  1409.3 1.4 copy.107
  1410.7 1.4 copy.108
  (211 shorter events, 37.7 us)
Async XLA Ops:
  7.2 490.9 %copy-start = (bf16[768,768]{1,0:T(8,128)(2,1)S(1)}, bf16[768,768]{1,0:T(8,128)(2,1)}, u32[]{:S(2)}) copy-start(bf16[768,768]{1,0:T(8,128)(2,1)} %param.31) | copy-start | bytes 3538948
  7.2 470.7 %all-gather.3.cloned.1.call-start = ((), (), s32[]{:S(2)}) async-start(), calls=%async_computation.3 | async-start | bytes 31457280 | tf_op jit(solution)/shard_map/all_gather | solution.py:107
  8.0 5.0 copy-start.25
  8.1 5.0 copy-start.28
  8.8 481.9 %copy-start.20 = (f32[2048]{0:T(1024)}, f32[2048]{0:T(1024)S(1)}, u32[]{:S(2)}) copy-start(f32[2048]{0:T(1024)S(1)} %convert_element_type.100) | copy-start | bytes 24580
  17.7 7.9 copy-start.22
  42.0 7.8 copy-start.7
  44.2 0.9 copy-start.5
  49.8 0.7 copy-start.35
  49.8 0.7 copy-start.36
  49.8 0.7 copy-start.37
  49.9 0.7 copy-start.38
  49.9 694.0 %all-reduce.7.cloned.1.call-start = ((), (), s32[]{:S(2)}) async-start(), calls=%async_computation | async-start | bytes 12582912 | tf_op jit(solution)/shard_map/psum | solution.py:116
  477.9 12.7 copy-start.26
  477.9 12.7 copy-start.29
  495.4 2.7 copy-start.1
  498.0 18.4 %copy-start.9 = (bf16[2048,768]{1,0:T(8,128)(2,1)}, bf16[2048,768]{1,0:T(8,128)(2,1)S(1)}, u32[]{:S(2)}) copy-start(bf16[2048,768]{1,0:T(8,128)(2,1)S(1)} %fusion.63) | copy-start | bytes 9437188
  498.0 20.1 %copy-start.42 = (bf16[768,768]{1,0:T(8,128)(2,1)S(1)}, bf16[768,768]{1,0:T(8,128)(2,1)}, u32[]{:S(2)}) copy-start(bf16[768,768]{1,0:T(8,128)(2,1)} %param.33) | copy-start | bytes 3538948
  516.5 1.6 copy-start.10
  522.7 0.7 copy-start.39
  522.7 0.7 copy-start.40
  522.7 0.7 copy-start.41
  522.7 474.6 %all-reduce.9.cloned.1.call-start = ((), (), s32[]{:S(2)}) async-start(), calls=%async_computation.1 | async-start | bytes 12582912 | tf_op jit(solution)/shard_map/psum | solution.py:137
  749.6 1.9 copy-start.4
  751.5 8.1 slice-start
  755.1 4.5 copy-start.43
  755.1 4.5 slice-start.1
  759.6 9.5 copy-start.3
  769.1 1.8 copy-start.44
  775.4 511.6 %all-reduce.11.cloned.1.call-start = ((), (), s32[]{:S(2)}) async-start(), calls=%async_computation.2 | async-start | bytes 12582912 | tf_op jit(solution)/shard_map/psum | solution.py:161
  1006.1 7.2 copy-start.15
  1010.6 2.7 copy-start.2
  1019.7 2.0 copy-start.18
  1020.9 1.5 copy-start.16
  1022.4 1.3 copy-start.19
  1022.8 0.9 copy-start.17
  1027.4 2.0 copy-start.18
  1028.6 1.5 copy-start.16
  1030.1 1.3 copy-start.19
  1030.5 0.9 copy-start.17
  1035.1 2.0 copy-start.18
  1036.3 1.5 copy-start.16
  1037.7 1.3 copy-start.19
  1038.2 0.9 copy-start.17
  1042.8 2.0 copy-start.18
  1044.0 1.5 copy-start.16
  1045.4 1.3 copy-start.19
  1045.8 0.9 copy-start.17
  1065.2 339.2 %all-reduce.13.cloned.1.call-start = ((), (), s32[]{:S(2)}) async-start(), calls=%async_computation.4 | async-start | bytes 14155776 | tf_op jit(solution)/shard_map/psum | solution.py:175
  1065.5 7.1 copy-start.11
  1072.6 7.1 copy-start.6
  1079.7 4.6 copy-start.8
  1079.7 4.6 copy-start.12
  1079.7 4.6 copy-start.21
  1079.7 4.6 copy-start.27
  1079.7 4.6 copy-start.30
  1088.1 205.9 %copy-start.23 = (f32[768]{0:T(1024)S(1)}, f32[768]{0:T(1024)}, u32[]{:S(2)}) copy-start(f32[768]{0:T(1024)} %get-tuple-element.150) | copy-start | bytes 9220
  1088.1 205.9 %copy-start.24 = (f32[768]{0:T(1024)S(1)}, f32[768]{0:T(1024)}, u32[]{:S(2)}) copy-start(f32[768]{0:T(1024)} %get-tuple-element.156) | copy-start | bytes 9220
  1088.1 205.9 %copy-start.31 = (f32[768]{0:T(1024)S(1)}, f32[768]{0:T(1024)}, u32[]{:S(2)}) copy-start(f32[768]{0:T(1024)} %get-tuple-element.208) | copy-start | bytes 9220
  1088.1 205.9 %copy-start.32 = (f32[768]{0:T(1024)S(1)}, f32[768]{0:T(1024)}, u32[]{:S(2)}) copy-start(f32[768]{0:T(1024)} %get-tuple-element.146) | copy-start | bytes 9220
  1088.1 205.9 %copy-start.33 = (f32[768]{0:T(1024)S(1)}, f32[768]{0:T(1024)}, u32[]{:S(2)}) copy-start(f32[768]{0:T(1024)} %get-tuple-element.153) | copy-start | bytes 9220
  1088.1 205.9 %copy-start.34 = (f32[768]{0:T(1024)S(1)}, f32[768]{0:T(1024)}, u32[]{:S(2)}) copy-start(f32[768]{0:T(1024)} %get-tuple-element.226) | copy-start | bytes 9220
  1404.4 4.9 copy-start.14
  1404.4 6.3 copy-start.13
Sparse Core Ops, SparseCore 0:
  50.0 427.8 all-gather.2
  522.8 221.0 all-reduce.6
  775.6 221.7 all-reduce.8
  1065.3 221.7 all-reduce.10
  1291.8 112.6 all-reduce.12
